TPU v7x, 32 devices: a whole 2x2x4 slice. The times are simulated.
32 devices in a mesh: seq: 8 (over y, x, core), tp: 4 (over z).
Axes of the slice: x: 2, y: 2, z: 4, core: 2. Of those that a mesh axis runs over, the one named last changes fastest.
Arguments:
- tokens: bfloat16 [128, 17, 1152], P('seq'), may hold values from -6 to 6
- cotangent: bfloat16 [128, 17, 1152], P('seq'), may hold values from -6 to 6
- caption: bfloat16 [4, 300, 1152], replicated, may hold values from -6 to 6
- condition: float32 [4, 1152], replicated, may hold values from -6 to 6
- frames: int32 [4], replicated, may hold values from 1 to 17, 44 in all
- cap_len: int32 [4], replicated, may hold values from 1 to 300, 600 in all
- clip_of: int32 [128], P('seq'), may hold values from 0 to 3
- w_qkv: bfloat16 [1152, 3, 1152], P('seq', None, 'tp'), may hold values from -0.1875 to 0.1875
- w_out: bfloat16 [1152, 1152], P('tp', 'seq'), may hold values from -0.375 to 0.375
- w_query2: bfloat16 [1152, 1152], P('seq', 'tp'), may hold values from -0.1875 to 0.1875
- w_kv2: bfloat16 [1152, 2, 1152], P('seq', None, 'tp'), may hold values from -0.1875 to 0.1875
- w_out2: bfloat16 [1152, 1152], P('tp', 'seq'), may hold values from -0.75 to 0.75
- w_up: bfloat16 [1152, 4608], P('seq', 'tp'), may hold values from -0.1875 to 0.1875
- w_down: bfloat16 [4608, 1152], P('tp', 'seq'), may hold values from -0.09375 to 0.09375
- w_ada: bfloat16 [1152, 6912], P('seq', 'tp'), may hold values from -0.1875 to 0.1875
Outputs:
- output: bfloat16 [128, 17, 1152], P('seq')
- d_tokens: bfloat16 [128, 17, 1152], P('seq')
- d_caption: float32 [4, 300, 1152], P(None, None, 'tp')
- d_condition: float32 [4, 1152], replicated
- d_w_qkv: float32 [1152, 3, 1152], P('seq', None, 'tp')
- d_w_out: float32 [1152, 1152], P('tp', 'seq')
- d_w_query2: float32 [1152, 1152], P('seq', 'tp')
- d_w_kv2: float32 [1152, 2, 1152], P('seq', None, 'tp')
- d_w_out2: float32 [1152, 1152], P('tp', 'seq')
- d_w_up: float32 [1152, 4608], P('seq', 'tp')
- d_w_down: float32 [4608, 1152], P('tp', 'seq')
- d_w_ada: float32 [1152, 6912], P('seq', 'tp')
Inputs may be any that keep to these rules, and one draw needn't show every extreme that they name: frames of each clip; they add up to 44 and one clip has 17. `cap_len`: live caption tokens of each clip, the first ones of its slots; they add up to 600 and one clip has 300.
All inputs are finite; a program needn't handle non-finite values.
Results may differ from a plain program's by a relative error of at most 0.024.
Values may be sent and summed in bfloat16 or wider, within the bound.
No kernel may reach another device: no remote copies, remote signals or barrier semaphores. Data moves between devices by JAX's collectives and lax.ppermute only.
A program may use at most 128 MiB of HBM per device.

v0:
```python
import jax
import jax.numpy as jnp
from jax import lax
from jax.sharding import PartitionSpec as P

HDIM = 72
CLIPS = 4


EPSILON = 1e-06
NEG_FILL = -1e30
HIGHEST = lax.Precision.HIGHEST


def normalize(rows):
    center = rows - jnp.mean(rows, -1, keepdims=True)
    return center * lax.rsqrt(jnp.mean(center * center, -1, keepdims=True) + EPSILON)


def modulate(rows, shift, scale):
    return normalize(rows) * (1.0 + scale[:, None, :]) + shift[:, None, :]


def total_rows(partial_value):
    return lax.psum(partial_value, "tp")


def frame_attention(triple, live, head_scale):
    raw = (
        jnp.einsum(
            "lfhe,lghe->lhfg", triple[:, :, 0], triple[:, :, 1], preferred_element_type=jnp.float32
        )
        * head_scale
    )
    probs = jax.nn.softmax(jnp.where(live[:, None, None, :], raw, NEG_FILL), axis=-1)
    result = jnp.einsum(
        "lhfg,lghe->lfhe",
        probs.astype(jnp.bfloat16),
        triple[:, :, 2],
        preferred_element_type=jnp.float32,
    )
    return (probs, result.astype(jnp.bfloat16))


def cross_scores(query, keys, clips, key_clip, key_live, head_scale):
    raw = jnp.einsum("rhe,khe->hrk", query, keys, preferred_element_type=jnp.float32) * head_scale
    allowed = (clips[:, None] == key_clip[None, :]) & key_live[None, :]
    return jnp.where(allowed[None], raw, NEG_FILL)


def shards(
    tokens,
    cotangent,
    caption,
    condition,
    frames,
    cap_len,
    clip_of,
    w_qkv,
    w_out,
    w_query2,
    w_kv2,
    w_out2,
    w_up,
    w_down,
    w_ada,
):
    seqs, fmax, width = tokens.shape
    row_count = seqs * fmax
    inner = w_qkv.shape[2]
    local_heads = inner // HDIM
    head_scale = HDIM ** (-0.5)
    full_qkv, full_out, full_query2, full_kv2, full_out2, full_up, full_down, full_ada = (
        lax.all_gather(w_qkv, "seq", axis=0, tiled=True),
        lax.all_gather(w_out, "seq", axis=1, tiled=True),
        lax.all_gather(w_query2, "seq", axis=0, tiled=True),
        lax.all_gather(w_kv2, "seq", axis=0, tiled=True),
        lax.all_gather(w_out2, "seq", axis=1, tiled=True),
        lax.all_gather(w_up, "seq", axis=0, tiled=True),
        lax.all_gather(w_down, "seq", axis=1, tiled=True),
        lax.all_gather(w_ada, "seq", axis=0, tiled=True),
    )
    qkv_matrix = full_qkv.reshape(width, 3 * inner)
    kv_matrix = full_kv2.reshape(width, 2 * inner)
    scaled = jax.nn.silu(condition).astype(jnp.bfloat16)
    mod_part = jnp.dot(scaled, full_ada, preferred_element_type=jnp.float32)
    mods = lax.all_gather(mod_part, "tp", axis=1, tiled=True).reshape(CLIPS, 6, width)
    clip_ids = jnp.arange(CLIPS)
    clip_hot = clip_of[:, None] == clip_ids[None, :]
    seq_mods = jnp.sum(jnp.where(clip_hot[:, :, None, None], mods[None], 0.0), 1)
    seq_frames = jnp.sum(jnp.where(clip_hot, frames[None, :], 0), 1)
    live = jnp.arange(fmax)[None, :] < seq_frames[:, None]
    own_live = live.astype(jnp.float32)[:, :, None]
    own_hot = clip_hot.astype(jnp.float32)
    key_count = caption.shape[0] * caption.shape[1]
    key_clip = jnp.arange(key_count) // caption.shape[1]
    key_len = jnp.sum(jnp.where(key_clip[:, None] == clip_ids[None, :], cap_len[None, :], 0), 1)
    key_live = jnp.arange(key_count) % caption.shape[1] < key_len
    row_clip = jnp.repeat(clip_of, fmax)
    block_seqs = min(32, seqs)
    blocks = seqs // block_seqs
    block_rows = block_seqs * fmax
    block_clip = row_clip.reshape(blocks, block_rows)
    own_input = tokens.astype(jnp.float32)
    attn_in = (
        modulate(own_input, seq_mods[:, 0], seq_mods[:, 1])
        .astype(jnp.bfloat16)
        .reshape(row_count, width)
    )
    triple = (
        jnp.dot(attn_in, qkv_matrix, preferred_element_type=jnp.float32)
        .astype(jnp.bfloat16)
        .reshape(seqs, fmax, 3, local_heads, HDIM)
    )
    probs, frame_out = frame_attention(triple, live, head_scale)
    frame_out = frame_out.reshape(row_count, inner)
    branch_one = total_rows(
        jnp.dot(frame_out, full_out, preferred_element_type=jnp.float32).reshape(seqs, fmax, width)
    )
    first = own_input + seq_mods[:, 2][:, None, :] * branch_one
    first_low = first.astype(jnp.bfloat16).reshape(row_count, width)
    cross_query = (
        jnp.dot(first_low, full_query2, preferred_element_type=jnp.float32)
        .astype(jnp.bfloat16)
        .reshape(blocks, block_rows, local_heads, HDIM)
    )
    cross_kv = (
        jnp.dot(caption.reshape(key_count, width), kv_matrix, preferred_element_type=jnp.float32)
        .astype(jnp.bfloat16)
        .reshape(key_count, 2, local_heads, HDIM)
    )
    cross_key = cross_kv[:, 0]
    cross_value = cross_kv[:, 1]

    def cross_block(pair):
        query, clips = pair
        scores = cross_scores(query, cross_key, clips, key_clip, key_live, head_scale)
        top = jnp.max(scores, -1, keepdims=True)
        weights = jnp.exp(scores - top)
        denom = jnp.sum(weights, -1, keepdims=True)
        block_out = jnp.einsum(
            "hrk,khe->rhe",
            (weights / denom).astype(jnp.bfloat16),
            cross_value,
            preferred_element_type=jnp.float32,
        )
        return (block_out.astype(jnp.bfloat16), (top + jnp.log(denom))[..., 0])

    cross_out, cross_lse = lax.map(cross_block, (cross_query, block_clip))
    cross_out = cross_out.reshape(row_count, inner)
    second = first + total_rows(
        jnp.dot(cross_out, full_out2, preferred_element_type=jnp.float32).reshape(seqs, fmax, width)
    )
    mlp_in = (
        modulate(second, seq_mods[:, 3], seq_mods[:, 4])
        .astype(jnp.bfloat16)
        .reshape(row_count, width)
    )
    hidden_pre = jnp.dot(mlp_in, full_up, preferred_element_type=jnp.float32)
    hidden = jax.nn.gelu(hidden_pre, approximate=True).astype(jnp.bfloat16)
    branch_three = total_rows(
        jnp.dot(hidden, full_down, preferred_element_type=jnp.float32).reshape(seqs, fmax, width)
    )
    third = second + seq_mods[:, 5][:, None, :] * branch_three
    output = (third * own_live).astype(jnp.bfloat16)
    grad_three = cotangent.astype(jnp.float32) * own_live
    d_branch3 = (
        (seq_mods[:, 5][:, None, :] * grad_three).astype(jnp.bfloat16).reshape(row_count, width)
    )
    grad_down = jnp.einsum("rk,rd->kd", hidden, d_branch3, preferred_element_type=jnp.float32)
    d_hidden = jnp.einsum("rd,kd->rk", d_branch3, full_down, preferred_element_type=jnp.float32)
    gelu_pull = jax.vjp(lambda value: jax.nn.gelu(value, approximate=True), hidden_pre)[1]
    d_pre = gelu_pull(d_hidden)[0].astype(jnp.bfloat16)
    grad_up = jnp.einsum("rd,rk->dk", mlp_in, d_pre, preferred_element_type=jnp.float32)
    d_mlp = total_rows(
        jnp.einsum("rk,dk->rd", d_pre, full_up, preferred_element_type=jnp.float32).reshape(
            seqs, fmax, width
        )
    )
    second_pull = jax.vjp(modulate, second, seq_mods[:, 3], seq_mods[:, 4])[1]
    norm_two, d_shift2, d_scale2 = second_pull(d_mlp)
    grad_two = grad_three + norm_two
    d_branch2 = grad_two.astype(jnp.bfloat16).reshape(row_count, width)
    grad_out2 = jnp.einsum("rc,rd->cd", cross_out, d_branch2, preferred_element_type=jnp.float32)
    d_cross = (
        jnp.einsum("rd,cd->rc", d_branch2, full_out2, preferred_element_type=jnp.float32)
        .astype(jnp.bfloat16)
        .reshape(blocks, block_rows, local_heads, HDIM)
    )

    def cross_back(carry, item):
        key_sum, value_sum = carry
        query, clips, block_lse, grad_block = item
        scores = cross_scores(query, cross_key, clips, key_clip, key_live, head_scale)
        weights = jnp.exp(scores - block_lse[..., None])
        value_sum = value_sum + jnp.einsum(
            "hrk,rhe->khe",
            weights.astype(jnp.bfloat16),
            grad_block,
            preferred_element_type=jnp.float32,
        )
        grad_weights = jnp.einsum(
            "rhe,khe->hrk", grad_block, cross_value, preferred_element_type=jnp.float32
        )
        grad_scores = (
            weights * (grad_weights - jnp.sum(weights * grad_weights, -1, keepdims=True))
        ).astype(jnp.bfloat16)
        grad_query = (
            jnp.einsum("hrk,khe->rhe", grad_scores, cross_key, preferred_element_type=jnp.float32)
            * head_scale
        ).astype(jnp.bfloat16)
        key_sum = (
            key_sum
            + jnp.einsum("hrk,rhe->khe", grad_scores, query, preferred_element_type=jnp.float32)
            * head_scale
        )
        return ((key_sum, value_sum), grad_query)

    zero_keys = jnp.zeros((key_count, local_heads, HDIM), jnp.float32)
    (key_grad, value_grad), d_query = lax.scan(
        cross_back, (zero_keys, zero_keys), (cross_query, block_clip, cross_lse, d_cross)
    )
    d_query = d_query.reshape(row_count, inner)
    grad_query2 = jnp.einsum("rd,rc->dc", first_low, d_query, preferred_element_type=jnp.float32)
    grad_one = grad_two + total_rows(
        jnp.einsum("rc,dc->rd", d_query, full_query2, preferred_element_type=jnp.float32).reshape(
            seqs, fmax, width
        )
    )
    d_branch1 = (
        (seq_mods[:, 2][:, None, :] * grad_one).astype(jnp.bfloat16).reshape(row_count, width)
    )
    grad_out = jnp.einsum("rc,rd->cd", frame_out, d_branch1, preferred_element_type=jnp.float32)
    d_frame = (
        jnp.einsum("rd,cd->rc", d_branch1, full_out, preferred_element_type=jnp.float32)
        .astype(jnp.bfloat16)
        .reshape(seqs, fmax, local_heads, HDIM)
    )
    d_value = jnp.einsum(
        "lhfg,lfhe->lghe", probs.astype(jnp.bfloat16), d_frame, preferred_element_type=jnp.float32
    )
    d_probs = jnp.einsum(
        "lfhe,lghe->lhfg", d_frame, triple[:, :, 2], preferred_element_type=jnp.float32
    )
    d_scores = (probs * (d_probs - jnp.sum(probs * d_probs, -1, keepdims=True))).astype(
        jnp.bfloat16
    )
    d_queries = (
        jnp.einsum("lhfg,lghe->lfhe", d_scores, triple[:, :, 1], preferred_element_type=jnp.float32)
        * head_scale
    )
    d_keys = (
        jnp.einsum("lhfg,lfhe->lghe", d_scores, triple[:, :, 0], preferred_element_type=jnp.float32)
        * head_scale
    )
    d_triple = (
        jnp.stack([d_queries, d_keys, d_value], 2)
        .astype(jnp.bfloat16)
        .reshape(row_count, 3 * inner)
    )
    grad_qkv = jnp.einsum(
        "rd,rc->dc", attn_in, d_triple, preferred_element_type=jnp.float32
    ).reshape(width, 3, inner)
    d_attn = total_rows(
        jnp.einsum("rc,dc->rd", d_triple, qkv_matrix, preferred_element_type=jnp.float32).reshape(
            seqs, fmax, width
        )
    )
    first_pull = jax.vjp(modulate, own_input, seq_mods[:, 0], seq_mods[:, 1])[1]
    norm_one, d_shift1, d_scale1 = first_pull(d_attn)
    d_tokens = (grad_one + norm_one).astype(jnp.bfloat16)
    d_gate1 = jnp.sum(grad_one * branch_one, 1)
    d_gate2 = jnp.sum(grad_three * branch_three, 1)
    seq_terms = jnp.stack([d_shift1, d_scale1, d_gate1, d_shift2, d_scale2, d_gate2], 1)
    d_mods = jnp.einsum("lc,ljd->cjd", own_hot, seq_terms, precision=HIGHEST).reshape(
        CLIPS, 6 * width
    )
    kv_grad = jnp.stack([key_grad, value_grad], 1)
    kv_total, mods_total = (
        lax.psum(kv_grad.astype(jnp.bfloat16), "seq").astype(jnp.float32),
        lax.psum(d_mods.astype(jnp.bfloat16), "seq").astype(jnp.float32),
    )
    col_count = mods_total.shape[1] // lax.axis_size("tp")
    mod_cols = lax.dynamic_slice_in_dim(mods_total, lax.axis_index("tp") * col_count, col_count, 1)
    seq_rows = w_ada.shape[0]
    seq_start = lax.axis_index("seq") * seq_rows
    scaled_rows = lax.dynamic_slice_in_dim(scaled, seq_start, seq_rows, 1).astype(jnp.float32)
    grad_ada = jnp.einsum("cd,ck->dk", scaled_rows, mod_cols, precision=HIGHEST)
    silu_pull = jax.vjp(jax.nn.silu, condition)[1]
    cond_part = silu_pull(
        jnp.einsum("ck,dk->cd", mod_cols, full_ada.astype(jnp.float32), precision=HIGHEST)
    )[0]
    d_condition = lax.psum(cond_part, "tp")
    kv_low = kv_total.astype(jnp.bfloat16).reshape(key_count, 2 * inner)
    caption_rows = lax.dynamic_slice_in_dim(
        caption.reshape(key_count, width), seq_start, seq_rows, 1
    )
    grad_kv2 = jnp.einsum(
        "kd,kc->dc", caption_rows, kv_low, preferred_element_type=jnp.float32
    ).reshape(seq_rows, 2, inner)
    caption_part = jnp.einsum(
        "kc,dc->kd", kv_low, kv_matrix, preferred_element_type=jnp.float32
    ).reshape(caption.shape)
    d_caption = lax.psum_scatter(
        caption_part.astype(jnp.bfloat16), "tp", scatter_dimension=2, tiled=True
    ).astype(jnp.float32)
    summed = (
        lax.psum_scatter(
            grad_qkv.astype(jnp.bfloat16), "seq", scatter_dimension=0, tiled=True
        ).astype(jnp.float32),
        lax.psum_scatter(
            grad_out.astype(jnp.bfloat16), "seq", scatter_dimension=1, tiled=True
        ).astype(jnp.float32),
        lax.psum_scatter(
            grad_query2.astype(jnp.bfloat16), "seq", scatter_dimension=0, tiled=True
        ).astype(jnp.float32),
        lax.psum_scatter(
            grad_out2.astype(jnp.bfloat16), "seq", scatter_dimension=1, tiled=True
        ).astype(jnp.float32),
        lax.psum_scatter(
            grad_up.astype(jnp.bfloat16), "seq", scatter_dimension=0, tiled=True
        ).astype(jnp.float32),
        lax.psum_scatter(
            grad_down.astype(jnp.bfloat16), "seq", scatter_dimension=1, tiled=True
        ).astype(jnp.float32),
    )
    return (
        output,
        d_tokens,
        d_caption,
        d_condition,
        summed[0],
        summed[1],
        summed[2],
        grad_kv2,
        summed[3],
        summed[4],
        summed[5],
        grad_ada,
    )


def solution(mesh):
    return jax.shard_map(
        shards,
        mesh=mesh,
        in_specs=(
            P("seq", None, None),
            P("seq", None, None),
            P(),
            P(),
            P(),
            P(),
            P("seq"),
            P("seq", None, "tp"),
            P("tp", "seq"),
            P("seq", "tp"),
            P("seq", None, "tp"),
            P("tp", "seq"),
            P("seq", "tp"),
            P("tp", "seq"),
            P("seq", "tp"),
        ),
        out_specs=(
            P("seq", None, None),
            P("seq", None, None),
            P(None, None, "tp"),
            P(),
            P("seq", None, "tp"),
            P("tp", "seq"),
            P("seq", "tp"),
            P("seq", None, "tp"),
            P("tp", "seq"),
            P("seq", "tp"),
            P("tp", "seq"),
            P("seq", "tp"),
        ),
        check_vma=False,
    )
```

profile of v0, /device:TPU:0, one launch (start us, length us, event | category | flops | bytes accessed | tf_op | source)
XLA Modules:
  0.0 1068.3 jit_solution(13612882484881826433)
XLA Ops:
  14.8 15.0 %all_gather.30 = bf16[288,1152]{0,1:T(8,128)(2,1)S(1)} all-gather(bf16[288,144]{0,1:T(8,128)(2,1)S(1)} %copy-done.45), channel_id=1, replica_groups=mesh['seq'=8,'tp'=4] {'seq'}, dimensions={1}, use_global_device_ids=true | all-gather | bytes 746496 | tf_op jit(solution)/shard_map/all_gather | solution.py:75
  29.7 13.7 %all_gather.32 = bf16[1152,288]{1,0:T(8,128)(2,1)S(1)} all-gather(bf16[144,288]{1,0:T(8,128)(2,1)S(1)} %copy-done.46), channel_id=1, replica_groups=mesh['seq'=8,'tp'=4] {'seq'}, dimensions={0}, use_global_device_ids=true | all-gather | bytes 746496 | tf_op jit(solution)/shard_map/all_gather | solution.py:76
  43.4 11.3 %all_gather.33 = bf16[288,1152]{0,1:T(8,128)(2,1)} all-gather(bf16[288,144]{0,1:T(8,128)(2,1)S(1)} %copy-done.47), channel_id=1, replica_groups=mesh['seq'=8,'tp'=4] {'seq'}, dimensions={1}, use_global_device_ids=true | all-gather | bytes 746496 | tf_op jit(solution)/shard_map/all_gather | solution.py:78
  64.2 21.8 %all-gather.7.cloned.1.call-done = bf16[1152,1728]{1,0:T(8,128)(2,1)} async-done(((bf16[144,1728]{1,0:T(8,128)(2,1)}), bf16[1152,1728]{1,0:T(8,128)(2,1)}) %all-gather.7.cloned.1.call-update) | async-done | bytes 3981328 | tf_op jit(solution)/shard_map/all_gather | solution.py:81
  88.8 13.4 %all-gather = f32[4,1728,4]{1,2,0:T(4,128)S(1)} all-gather(f32[1,1728,4]{1,2,0:T(4,128)S(1)} %convolution_bitcast_fusion), channel_id=1, replica_groups=mesh['seq'=8,'tp'=4] {'tp'}, dimensions={0}, use_global_device_ids=true | all-gather | bytes 138240 | tf_op jit(solution)/shard_map/all_gather | solution.py:87
  123.6 5.6 copy.152
  129.2 5.5 convolution_convert_fusion.4
  134.8 63.0 %all-reduce.8.cloned.1.call-done = f32[16,17,1152]{2,1,0:T(8,128)} async-done(((f32[16,17,1152]{2,1,0:T(8,128)}), f32[16,17,1152]{2,1,0:T(8,128)}) %all-reduce.8.cloned.1.call-update) | async-done | bytes 1253392 | tf_op jit(solution)/shard_map/psum | solution.py:25
  212.2 73.4 %all-reduce.10.cloned.1.call-done = f32[16,17,1152]{2,1,0:T(8,128)} async-done(((f32[16,17,1152]{2,1,0:T(8,128)}), f32[16,17,1152]{2,1,0:T(8,128)}) %all-reduce.10.cloned.1.call-update) | async-done | bytes 1253392 | tf_op jit(solution)/shard_map/psum | solution.py:25
  295.4 21.2 %all-gather.15.cloned.1.call-done = bf16[1152,1152]{0,1:T(8,128)(2,1)} async-done(((bf16[1152,144]{0,1:T(8,128)(2,1)}), bf16[1152,1152]{0,1:T(8,128)(2,1)}) %all-gather.15.cloned.1.call-update) | async-done | bytes 2654224 | tf_op jit(solution)/shard_map/all_gather | solution.py:80
  320.6 28.1 %all-gather.13.cloned.1.call-done = bf16[1152,1152]{1,0:T(8,128)(2,1)} async-done(((bf16[144,1152]{1,0:T(8,128)(2,1)}), bf16[1152,1152]{1,0:T(8,128)(2,1)}) %all-gather.13.cloned.1.call-update) | async-done | bytes 2654224 | tf_op jit(solution)/shard_map/all_gather | solution.py:79
  348.8 5.0 fusion.36
  359.7 75.4 %all-reduce.12.cloned.1.call-done = f32[16,17,1152]{2,1,0:T(8,128)} async-done(((f32[16,17,1152]{2,1,0:T(8,128)}), f32[16,17,1152]{2,1,0:T(8,128)}) %all-reduce.12.cloned.1.call-update) | async-done | bytes 1253392 | tf_op jit(solution)/shard_map/psum | solution.py:25
  476.0 59.8 %all-reduce.14.cloned.1.call-done = f32[16,17,1152]{2,1,0:T(8,128)} async-done(((f32[16,17,1152]{2,1,0:T(8,128)}), f32[16,17,1152]{2,1,0:T(8,128)}) %all-reduce.14.cloned.1.call-update) | async-done | bytes 1253392 | tf_op jit(solution)/shard_map/psum | solution.py:25
  604.4 6.6 convolution_convert_fusion.2
  611.0 23.5 %reduce-scatter.16.cloned.1.call-done = bf16[288,144]{0,1:T(8,128)(2,1)} async-done(((bf16[288,1152]{0,1:T(8,128)(2,1)}), bf16[288,144]{0,1:T(8,128)(2,1)}) %reduce-scatter.16.cloned.1.call-update) | async-done | bytes 82960 | tf_op jit(solution)/shard_map/reduce_scatter | solution.py:317
  636.1 36.6 %reduce-scatter.14.cloned.1.call-done = bf16[144,288]{1,0:T(8,128)(2,1)} async-done(((bf16[1152,288]{1,0:T(8,128)(2,1)}), bf16[144,288]{1,0:T(8,128)(2,1)}) %reduce-scatter.14.cloned.1.call-update) | async-done | bytes 82960 | tf_op jit(solution)/shard_map/reduce_scatter | solution.py:314
  674.3 37.6 %reduce-scatter.12.cloned.1.call-done = bf16[288,144]{0,1:T(8,128)(2,1)} async-done(((bf16[288,1152]{0,1:T(8,128)(2,1)}), bf16[288,144]{0,1:T(8,128)(2,1)}) %reduce-scatter.12.cloned.1.call-update) | async-done | bytes 82960 | tf_op jit(solution)/shard_map/reduce_scatter | solution.py:311
  713.5 45.6 %reduce-scatter.18.cloned.1.call-done = bf16[144,1152]{1,0:T(8,128)(2,1)} async-done(((bf16[1152,1152]{1,0:T(8,128)(2,1)}), bf16[144,1152]{1,0:T(8,128)(2,1)}) %reduce-scatter.18.cloned.1.call-update) | async-done | bytes 331792 | tf_op jit(solution)/shard_map/reduce_scatter | solution.py:320
  760.9 45.7 %reduce-scatter.20.cloned.1.call-done = bf16[1152,144]{0,1:T(8,128)(2,1)} async-done(((bf16[1152,1152]{0,1:T(8,128)(2,1)}), bf16[1152,144]{0,1:T(8,128)(2,1)}) %reduce-scatter.20.cloned.1.call-update) | async-done | bytes 331792 | tf_op jit(solution)/shard_map/reduce_scatter | solution.py:323
  808.4 135.2 %all-reduce.18.cloned.1.call-done = (f32[16,17,1152]{2,1,0:T(8,128)}, f32[16,17,1152]{2,1,0:T(8,128)}) async-done(((f32[16,17,1152]{2,1,0:T(8,128)}, f32[16,17,1152]{2,1,0:T(8,128)}), (f32[16,17,1152]{2,1,0:T(8,128)}, f32[16,17,1152]{2,1,0:T(8,128)})) %all-reduce.18.cloned.1.call-update) | async-done | bytes 2506768 | tf_op jit(solution)/shard_map/psum | solution.py:25
  951.0 24.9 %psum.70 = bf16[4,6912]{1,0:T(4,128)(2,1)S(1)} all-reduce(bf16[4,6912]{1,0:T(4,128)(2,1)S(1)} %bitcast.198), channel_id=1, replica_groups=mesh['seq'=8,'tp'=4] {'seq'}, use_global_device_ids=true, to_apply=%region_31.32 | all-reduce | flops 27648 | bytes 110592 | tf_op jit(solution)/shard_map/psum | solution.py:281
  979.3 17.6 %psum.71 = f32[4,1152]{1,0:T(4,128)} all-reduce(f32[4,1152]{1,0:T(4,128)S(1)} %fusion.68), channel_id=1, replica_groups=mesh['seq'=8,'tp'=4] {'tp'}, use_global_device_ids=true, to_apply=%region_32.33 | all-reduce | flops 4608 | bytes 36864 | tf_op jit(solution)/shard_map/psum | solution.py:293
  1000.8 57.7 %reduce-scatter.8.cloned.1.call-done = bf16[4,300,288]{1,2,0:T(8,128)(2,1)} async-done(((bf16[4,300,1152]{1,2,0:T(8,128)(2,1)}), bf16[4,300,288]{1,2,0:T(8,128)(2,1)}) %reduce-scatter.8.cloned.1.call-update) | async-done | bytes 691216 | tf_op jit(solution)/shard_map/reduce_scatter | solution.py:304
  (301 shorter events, 209.5 us)
Async XLA Ops:
  7.2 52.7 %all-gather.9.cloned.1.call-start = ((), (), s32[]{:S(2)}) async-start(), calls=%async_computation.8 | async-start | bytes 2985984 | tf_op jit(solution)/shard_map/all_gather | solution.py:74
  8.0 78.0 %all-gather.7.cloned.1.call-start = ((), (), s32[]{:S(2)}) async-start(), calls=%async_computation.7 | async-start | bytes 4644864 | tf_op jit(solution)/shard_map/all_gather | solution.py:81
  8.7 114.9 %all-gather.11.cloned.1.call-start = ((), (), s32[]{:S(2)}) async-start(), calls=%async_computation.10 | async-start | bytes 1990656 | tf_op jit(solution)/shard_map/all_gather | solution.py:77
  9.5 188.3 %all-reduce.8.cloned.1.call-start = ((), (), s32[]{:S(2)}) async-start(), calls=%async_computation.9 | async-start | bytes 3538944 | tf_op jit(solution)/shard_map/psum | solution.py:25
  29.7 90.2 %copy-start.9 = (bf16[288,1152]{0,1:T(8,128)(2,1)}, bf16[288,1152]{0,1:T(8,128)(2,1)S(1)}, u32[]{:S(2)}) copy-start(bf16[288,1152]{0,1:T(8,128)(2,1)S(1)} %all_gather.30) | copy-start | bytes 1990660
  43.4 156.4 %copy-start.10 = (bf16[1152,288]{1,0:T(8,128)(2,1)}, bf16[1152,288]{1,0:T(8,128)(2,1)S(1)}, u32[]{:S(2)}) copy-start(bf16[1152,288]{1,0:T(8,128)(2,1)S(1)} %all_gather.32) | copy-start | bytes 1990660
  103.3 182.3 %copy-start.31 = (f32[16,1152]{1,0:T(8,128)}, f32[16,1152]{1,0:T(8,128)S(1)}, u32[]{:S(2)}) copy-start(f32[16,1152]{1,0:T(8,128)S(1)} %get-tuple-element.159) | copy-start | bytes 221188
  103.3 185.1 %copy-start.36 = (f32[16,1152]{1,0:T(8,128)}, f32[16,1152]{1,0:T(8,128)S(1)}, u32[]{:S(2)}) copy-start(f32[16,1152]{1,0:T(8,128)S(1)} %get-tuple-element.154) | copy-start | bytes 221188
  121.9 163.6 %all-reduce.10.cloned.1.call-start = ((), (), s32[]{:S(2)}) async-start(), calls=%async_computation.11 | async-start | bytes 3538944 | tf_op jit(solution)/shard_map/psum | solution.py:25
  210.8 105.8 %all-gather.15.cloned.1.call-start = ((), (), s32[]{:S(2)}) async-start(), calls=%async_computation.13 | async-start | bytes 2985984 | tf_op jit(solution)/shard_map/all_gather | solution.py:80
  211.4 137.4 %all-gather.13.cloned.1.call-start = ((), (), s32[]{:S(2)}) async-start(), calls=%async_computation.12 | async-start | bytes 2985984 | tf_op jit(solution)/shard_map/all_gather | solution.py:79
  212.1 223.0 %all-reduce.12.cloned.1.call-start = ((), (), s32[]{:S(2)}) async-start(), calls=%async_computation.14 | async-start | bytes 3538944 | tf_op jit(solution)/shard_map/psum | solution.py:25
  359.5 176.3 %all-reduce.14.cloned.1.call-start = ((), (), s32[]{:S(2)}) async-start(), calls=%async_computation.15 | async-start | bytes 3538944 | tf_op jit(solution)/shard_map/psum | solution.py:25
  461.1 135.5 %all-reduce.16.cloned.1.call-start = ((), (), s32[]{:S(2)}) async-start(), calls=%async_computation.16 | async-start | bytes 2949120 | tf_op jit(solution)/shard_map/psum | solution.py:280
  469.2 165.3 %reduce-scatter.16.cloned.1.call-start = ((), (), s32[]{:S(2)}) async-start(), calls=%async_computation.21 | async-start | bytes 995328 | tf_op jit(solution)/shard_map/reduce_scatter | solution.py:317
  472.2 200.5 %reduce-scatter.14.cloned.1.call-start = ((), (), s32[]{:S(2)}) async-start(), calls=%async_computation.20 | async-start | bytes 995328 | tf_op jit(solution)/shard_map/reduce_scatter | solution.py:314
  475.9 236.0 %reduce-scatter.12.cloned.1.call-start = ((), (), s32[]{:S(2)}) async-start(), calls=%async_computation.19 | async-start | bytes 995328 | tf_op jit(solution)/shard_map/reduce_scatter | solution.py:311
  546.9 212.1 %reduce-scatter.18.cloned.1.call-start = ((), (), s32[]{:S(2)}) async-start(), calls=%async_computation.22 | async-start | bytes 2985984 | tf_op jit(solution)/shard_map/reduce_scatter | solution.py:320
  551.7 254.9 %reduce-scatter.20.cloned.1.call-start = ((), (), s32[]{:S(2)}) async-start(), calls=%async_computation.23 | async-start | bytes 2985984 | tf_op jit(solution)/shard_map/reduce_scatter | solution.py:323
  556.5 387.1 %all-reduce.18.cloned.1.call-start = ((), (), s32[]{:S(2)}) async-start(), calls=%async_computation.24 | async-start | bytes 7077888 | tf_op jit(solution)/shard_map/psum | solution.py:25
  581.7 417.3 %reduce-scatter.10.cloned.1.call-start = ((), (), s32[]{:S(2)}) async-start(), calls=%async_computation.18 | async-start | bytes 2985984 | tf_op jit(solution)/shard_map/reduce_scatter | solution.py:308
  591.7 466.9 %reduce-scatter.8.cloned.1.call-start = ((), (), s32[]{:S(2)}) async-start(), calls=%async_computation.17 | async-start | bytes 4423680 | tf_op jit(solution)/shard_map/reduce_scatter | solution.py:304
  611.0 332.6 %copy-start.23 = (f32[16,1152]{1,0:T(8,128)S(1)}, f32[16,1152]{1,0:T(8,128)}, u32[]{:S(2)}) copy-start(f32[16,1152]{1,0:T(8,128)} %copy-done.22) | copy-start | bytes 221188
  760.9 184.8 %copy-start.51 = (f32[16,17]{1,0:T(8,128)S(1)}, f32[16,17]{1,0:T(8,128)}, u32[]{:S(2)}) copy-start(f32[16,17]{1,0:T(8,128)} %copy-done.50) | copy-start | bytes 3268
  (60 other events, 466.4 us)
Sparse Core Ops, SparseCore 0:
  10.0 37.6 all-gather.8
  49.5 36.4 all-gather.6
  87.9 26.5 all-gather.10
  122.0 75.7 all-reduce.7
  210.9 74.5 all-reduce.9
  287.3 29.2 all-gather.14
  318.5 30.2 all-gather.12
  359.6 75.5 all-reduce.11
  461.2 74.5 all-reduce.13
  538.9 57.6 all-reduce.15
  600.1 34.3 reduce-scatter.15
  637.6 35.0 reduce-scatter.13
  676.8 35.0 reduce-scatter.11
  715.2 43.7 reduce-scatter.17
  762.8 43.7 reduce-scatter.19
  809.4 134.1 all-reduce.17
  947.0 42.9 reduce-scatter.9
  992.2 66.3 reduce-scatter.7
where the time goes:
time: 1080 us; the launch traced here: 1070 us
  waiting for transfers between devices  733 us (68%)
  matrix products  105 us (10%)
  blocking collectives  95.8 us (9%)
  local copies, waits for them, and re-layouts  71.9 us (7%)
  other arithmetic  45.7 us (4%)
  between operations  15.7 us (1%)
    psum x5, waiting for transfers between devices, total_rows(): return lax.psum(partial_value, 'tp')  407 us
    reduce_scatter x1, waiting for transfers between devices, shards(): lax.psum_scatter(caption_part.astype(jnp.bfloat16), 'tp', scatter_dimensi...  57.7 us
    reduce_scatter x1, waiting for transfers between devices, shards(): lax.psum_scatter(grad_down.astype(jnp.bfloat16), 'seq', scatter_dimension...  45.7 us
    reduce_scatter x1, waiting for transfers between devices, shards(): lax.psum_scatter(grad_up.astype(jnp.bfloat16), 'seq', scatter_dimension=0...  45.6 us
    reduce_scatter x1, waiting for transfers between devices, shards(): lax.psum_scatter(grad_out.astype(jnp.bfloat16), 'seq', scatter_dimension=...  37.6 us
    reduce_scatter x1, waiting for transfers between devices, shards(): lax.psum_scatter(grad_query2.astype(jnp.bfloat16), 'seq', scatter_dimensi...  36.6 us
    all_gather x1, waiting for transfers between devices, shards(): lax.all_gather(w_up, 'seq', axis=0, tiled=True)  28.1 us
    psum x1, blocking collectives, shards(): lax.psum(d_mods.astype(jnp.bfloat16), 'seq').astype(jnp.float32)  24.9 us
  transfers between devices with their start and end apart: 18, of which 15 were waited for; matrix products, arithmetic and copies ran while one was open for 15% of the time, Pallas kernels for 0%

commit v1 on v0

v1 whole, which is shorter than its diff:
```python
import functools

import jax
import jax.numpy as jnp
from jax import lax
from jax.experimental import pallas as pl
from jax.experimental.pallas import tpu as pltpu
from jax.sharding import PartitionSpec as P

HDIM = 72
EPSILON = 1e-06
NEG_FILL = -1e30
F32 = jnp.float32
BF16 = jnp.bfloat16
SCALE = HDIM ** (-0.5)
VMEM_LIMIT = 48 << 20


def dot_nn(a, b):
    return lax.dot_general(a, b, (((1,), (0,)), ((), ())), preferred_element_type=F32)


def dot_nt(a, b):
    return lax.dot_general(a, b, (((1,), (1,)), ((), ())), preferred_element_type=F32)


def dot_tn(a, b):
    return lax.dot_general(a, b, (((0,), (0,)), ((), ())), preferred_element_type=F32)


def call(body, outs, *args, name, specs=None, flops=0):
    vmem = pl.BlockSpec(memory_space=pltpu.VMEM)
    in_specs = [vmem] * len(args) if specs is None else [vmem if s is None else s for s in specs]
    moved = sum(a.size * a.dtype.itemsize for a in args)
    moved += sum(o.size * o.dtype.itemsize for o in outs)
    return pl.pallas_call(
        body,
        out_shape=tuple(outs),
        in_specs=in_specs,
        out_specs=tuple(vmem for _ in outs),
        compiler_params=pltpu.CompilerParams(vmem_limit_bytes=VMEM_LIMIT),
        cost_estimate=pl.CostEstimate(flops=flops, transcendentals=0, bytes_accessed=moved),
        name=name,
    )(*args)


def sds(shape, dtype=BF16):
    return jax.ShapeDtypeStruct(shape, dtype)


def norm_parts(rows):
    center = rows - jnp.mean(rows, -1, keepdims=True)
    inv = lax.rsqrt(jnp.mean(center * center, -1, keepdims=True) + EPSILON)
    return center * inv, inv


def expand(hot, table):
    high = table.astype(BF16)
    low = (table - high.astype(F32)).astype(BF16)
    return dot_nn(hot, high) + dot_nn(hot, low)


def clip_sums(hot, values):
    return dot_tn(hot, values.astype(BF16))


def norm_back(grad, n, inv):
    return inv * (grad - jnp.mean(grad, -1, keepdims=True) - n * jnp.mean(grad * n, -1, keepdims=True))


def softmax_rows(scores):
    top = jnp.max(scores, -1, keepdims=True)
    weights = jnp.exp(scores - top)
    return weights / jnp.sum(weights, -1, keepdims=True)


def pack_rows(out_ref, value, tp):
    own, n = value.shape[0] // tp, value.shape[1]
    for r in range(tp):
        out_ref[:, r * n : (r + 1) * n] = value[r * own : (r + 1) * own]


def unpack_heads(pieces, tp, n):
    rows = []
    for b in range(tp):
        cols = []
        for k in range(tp):
            r = (b - k) % tp
            cols.append(pieces[k][:, r * n : (r + 1) * n])
        rows.append(jnp.concatenate(cols, axis=1))
    return jnp.concatenate(rows, axis=0)


def frame_forward(tp, tok, hot, mods, row_id, key_id, w_qkv, attn_o, qkv_o, prob_o, fo_o, pack_o):
    n, _ = norm_parts(tok[...].astype(F32))
    low = (n * (1.0 + expand(hot[...], mods[1])) + expand(hot[...], mods[0])).astype(BF16)
    attn_o[...] = low
    qkv = dot_nn(low, w_qkv[...]).astype(BF16)
    qkv_o[...] = qkv
    inner = qkv.shape[1] // 3
    allowed = row_id[...] == key_id[...]
    outs = []
    for h in range(inner // HDIM):
        q, k, v = (qkv[:, i * inner + h * HDIM : i * inner + (h + 1) * HDIM] for i in range(3))
        probs = softmax_rows(jnp.where(allowed, dot_nt(q, k) * SCALE, NEG_FILL)).astype(BF16)
        prob_o[h] = probs
        outs.append(dot_nn(probs, v).astype(BF16))
    result = jnp.concatenate(outs, axis=1)
    fo_o[...] = result
    pack_rows(pack_o, result, tp)


def key_values(cap, w_kv, kv_o):
    kv_o[...] = dot_nn(cap[...], w_kv[...]).astype(BF16)


def cross_forward(tp, inner, *refs):
    pieces = [r[...] for r in refs[:tp]]
    tok, hot, mods, row_clip, key_clip, w_b, kv = refs[tp : tp + 7]
    x1_o, low_o, own_o, cq_o, prob_o, co_o, pack_o = refs[tp + 7 :]
    own, width = own_o.shape
    branch = dot_nt(unpack_heads(pieces, tp, inner), w_b[:, :width])
    own_o[...] = branch[:own]
    first = tok[...].astype(F32) + expand(hot[...], mods[2]) * branch
    x1_o[...] = first
    low = first.astype(BF16)
    low_o[...] = low
    cq = dot_nn(low, w_b[:, width + 2 * inner : width + 3 * inner]).astype(BF16)
    cq_o[...] = cq
    allowed = row_clip[...] == key_clip[...]
    outs = []
    for h in range(inner // HDIM):
        cols = slice(h * HDIM, (h + 1) * HDIM)
        key = kv[:, h * HDIM : (h + 1) * HDIM]
        value = kv[:, inner + h * HDIM : inner + (h + 1) * HDIM]
        scores = jnp.where(allowed, dot_nt(cq[:, cols], key) * SCALE, NEG_FILL)
        probs = softmax_rows(scores).astype(BF16)
        prob_o[h] = probs
        outs.append(dot_nn(probs, value).astype(BF16))
    result = jnp.concatenate(outs, axis=1)
    co_o[...] = result
    pack_rows(pack_o, result, tp)


GELU_C = 0.7978845608028654


def mlp_both(tp, inner, *refs):
    pieces = [r[...] for r in refs[:tp]]
    first, cot, live, hot, mods, w_c = refs[tp : tp + 6]
    outs = refs[tp + 6 :]
    x2_o, mlp_o, hid_o, db3_o, dpre_o = outs[:5]
    b3_o, dm_o = outs[5 : 5 + tp], outs[5 + tp :]
    own, width = x2_o.shape
    hid = hid_o.shape[1]
    w_up, w_down = w_c[:, width : width + hid], w_c[:, width + hid :]
    second = first[...] + dot_nt(unpack_heads(pieces, tp, inner), w_c[:, :width])
    x2_o[...] = second[:own]
    n, _ = norm_parts(second)
    low = (n * (1.0 + expand(hot[...], mods[4])) + expand(hot[...], mods[3])).astype(BF16)
    mlp_o[...] = low
    pre = dot_nn(low, w_up)
    inside = GELU_C * (pre + 0.044715 * (pre * pre * pre))
    th = jnp.tanh(inside)
    hidden = (0.5 * pre * (1.0 + th)).astype(BF16)
    hid_o[...] = hidden
    d_b3 = (expand(hot[...], mods[5]) * (cot[...].astype(F32) * live[...])).astype(BF16)
    db3_o[...] = d_b3
    slope = 0.5 * (1.0 + th) + 0.5 * pre * (1.0 - th * th) * (
        GELU_C * (1.0 + 3.0 * 0.044715 * (pre * pre))
    )
    d_pre = (slope * dot_nn(d_b3, w_down)).astype(BF16)
    dpre_o[...] = d_pre
    d_m = dot_nt(d_pre, w_up).astype(BF16)
    for r in range(tp):
        dm_o[r][...] = d_m[r * own : (r + 1) * own]
    b3 = dot_nt(hidden, w_down).astype(BF16)
    for r in range(tp):
        b3_o[r][...] = b3[r * own : (r + 1) * own]


def second_back(tp, *refs):
    d_m = refs[0][...].astype(F32)
    for r in refs[1:tp]:
        d_m = d_m + r[...].astype(F32)
    x2, cot, live, hot, mods, g2_o, db2_o, sums_o = refs[tp:]
    n, inv = norm_parts(x2[...])
    grad = d_m * (1.0 + expand(hot[...], mods[4]))
    g2 = cot[...].astype(F32) * live[...] + norm_back(grad, n, inv)
    g2_o[...] = g2
    db2_o[...] = g2.astype(BF16)
    sums_o[0] = clip_sums(hot[...], d_m)
    sums_o[1] = clip_sums(hot[...], d_m * n)


def out_rows(tp, *refs):
    b3 = refs[0][...].astype(F32)
    for r in refs[1:tp]:
        b3 = b3 + r[...].astype(F32)
    x2, cot, live, hot, mods, out_o, sums_o = refs[tp:]
    third = x2[...] + expand(hot[...], mods[5]) * b3
    out_o[...] = (third * live[...]).astype(BF16)
    sums_o[...] = clip_sums(hot[...], cot[...].astype(F32) * live[...] * b3)


def cross_back(tp, inner, *refs):
    d_b2 = jnp.concatenate([r[...] for r in refs[:tp]], axis=0)
    w_out2, prob, kv, cq, db2_o, dcq_o, dkv_o, pack_o = refs[tp:]
    db2_o[...] = d_b2
    d_co = dot_nn(d_b2, w_out2[...]).astype(BF16)
    d_q, d_k, d_v = [], [], []
    for h in range(inner // HDIM):
        cols = slice(h * HDIM, (h + 1) * HDIM)
        key = kv[:, h * HDIM : (h + 1) * HDIM]
        value = kv[:, inner + h * HDIM : inner + (h + 1) * HDIM]
        probs = prob[h]
        d_v.append(dot_tn(probs, d_co[:, cols]).astype(BF16))
        d_p = dot_nt(d_co[:, cols], value)
        wide = probs.astype(F32)
        d_s = (wide * (d_p - jnp.sum(wide * d_p, -1, keepdims=True))).astype(BF16)
        d_q.append((dot_nn(d_s, key) * SCALE).astype(BF16))
        d_k.append((dot_tn(d_s, cq[:, cols]) * SCALE).astype(BF16))
    result = jnp.concatenate(d_q, axis=1)
    dcq_o[...] = result
    pack_rows(pack_o, result, tp)
    dkv_o[...] = jnp.concatenate(d_k + d_v, axis=1)


def frame_back(tp, inner, *refs):
    pieces = [r[...] for r in refs[:tp]]
    rest = refs[tp:]
    d_b2, g2, own_b1, tok, hot, mods, w_b, w_q2, w_qkv, qkv, prob = rest[:11]
    outs = rest[11:]
    g1_o, db1_o, dqkv_o, sums_o = outs[:4]
    da_o = outs[4:]
    own, width = g1_o.shape
    d_cq = unpack_heads(pieces, tp, inner)
    d_x1 = dot_nt(d_cq[:, :inner], w_b[:, width + 2 * inner : width + 3 * inner]) + dot_nt(d_cq[:, inner:], w_q2[...])
    g1_own = g2[...] + d_x1[:own]
    g1_o[...] = g1_own
    d_b1 = (expand(hot[...], mods[2]) * (d_b2[...].astype(F32) + d_x1)).astype(BF16)
    db1_o[...] = d_b1
    d_fo = dot_nn(d_b1, w_b[:, :inner]).astype(BF16)
    d_q, d_k, d_v = [], [], []
    for h in range(inner // HDIM):
        q, k, v = (qkv[:, i * inner + h * HDIM : i * inner + (h + 1) * HDIM] for i in range(3))
        grad = d_fo[:, h * HDIM : (h + 1) * HDIM]
        probs = prob[h]
        d_v.append(dot_tn(probs, grad).astype(BF16))
        d_p = dot_nt(grad, v)
        wide = probs.astype(F32)
        d_s = (wide * (d_p - jnp.sum(wide * d_p, -1, keepdims=True))).astype(BF16)
        d_q.append((dot_nn(d_s, k) * SCALE).astype(BF16))
        d_k.append((dot_tn(d_s, q) * SCALE).astype(BF16))
    d_qkv = jnp.concatenate(d_q + d_k + d_v, axis=1)
    dqkv_o[...] = d_qkv
    d_a = dot_nt(d_qkv, w_qkv[...])
    low = d_a.astype(BF16)
    for r in range(tp):
        da_o[r][...] = low[r * own : (r + 1) * own]
    n, _ = norm_parts(tok[...].astype(F32))
    sums_o[0] = dot_tn(hot[...], low)
    sums_o[1] = clip_sums(hot[...], d_a * n)
    sums_o[2] = clip_sums(hot[:own], g1_own * own_b1[...])


def token_rows(tp, *refs):
    d_a = refs[0][...].astype(F32)
    for r in refs[1:tp]:
        d_a = d_a + r[...].astype(F32)
    tok, g1, hot, mods, out_o = refs[tp:]
    n, inv = norm_parts(tok[...].astype(F32))
    grad = d_a * (1.0 + expand(hot[...], mods[1]))
    out_o[...] = (g1[...] + norm_back(grad, n, inv)).astype(BF16)


def weight_grads(*refs):
    out_o = refs[-1]
    start = 0
    for i in range(0, len(refs) - 1, 2):
        width = refs[i + 1].shape[1]
        out_o[:, start : start + width] = dot_tn(refs[i][...], refs[i + 1][...]).astype(BF16)
        start += width


def weight_grads_relative(rank, *refs):
    out_o = refs[-1]
    blocks, size = out_o.shape[0], out_o.shape[1]
    start = 0
    for i in range(0, len(refs) - 1, 2):
        width = refs[i + 1].shape[1]
        grads = dot_tn(refs[i][...], refs[i + 1][...]).astype(BF16)
        for s in range(blocks):
            other = lax.bitwise_xor(rank[0], s)
            place = (other % 2) * (blocks // 2) + other // 2
            out_o[place, :, start : start + width] = grads[s * size : (s + 1) * size]
        start += width


def caption_rows(tp, rank, dkv, w_kv, out_o):
    size = out_o.shape[2]
    for r in range(tp):
        block = lax.rem(rank[0] - r + tp, tp)
        rows = w_kv[pl.ds(pl.multiple_of(block * size, size), size), :]
        out_o[r] = dot_nt(dkv[...], rows).astype(BF16)


def tp_gather(value, tp):
    return [value] + [
        lax.ppermute(value, "tp", [(i, (i + k) % tp) for i in range(tp)]) for k in range(1, tp)
    ]


def tp_scatter(chunks, tp):
    return [chunks[0]] + [
        lax.ppermute(chunks[r], "tp", [(i, (i - r) % tp) for i in range(tp)]) for r in range(1, tp)
    ]


def seq_xor(value, mask, nseq):
    return lax.ppermute(value, "seq", [(i, i ^ mask) for i in range(nseq)])


def seq_total(value, nseq):
    mask = 1
    while mask < nseq:
        value = value + seq_xor(value, mask, nseq)
        mask *= 2
    return value


def padded(value, size, axis):
    if value.shape[axis] == size:
        return value
    pads = [(0, 0)] * value.ndim
    pads[axis] = (0, size - value.shape[axis])
    return jnp.pad(value, pads)


def shards(
    tokens,
    cotangent,
    caption,
    condition,
    frames,
    cap_len,
    clip_of,
    w_qkv,
    w_out,
    w_query2,
    w_kv2,
    w_out2,
    w_up,
    w_down,
    w_ada,
):
    tp, nseq = lax.axis_size("tp"), lax.axis_size("seq")
    me, spot = lax.axis_index("tp"), lax.axis_index("seq")
    seqs, fmax, width = tokens.shape
    clips, slots = caption.shape[:2]
    inner, hid = w_query2.shape[1], w_up.shape[1]
    heads = inner // HDIM
    drows = w_query2.shape[0]
    own_seqs = seqs // tp
    own = -(-own_seqs * fmax // 8) * 8
    rows = tp * own
    clip_pad = 8
    keys = -(-(clips * slots // 2) // 128) * 128

    z_pack = jnp.concatenate([w_out.T, w_query2, w_out2.T], axis=1)
    z_parts = tp_gather(z_pack, tp)
    z_out, z_q2, z_out2 = (
        [p[:, i * inner : (i + 1) * inner] for p in z_parts] for i in range(3)
    )
    section = padded(jnp.concatenate([w_kv2.reshape(drows, 2 * inner), w_query2], 1), width, 1)
    pack_a = w_qkv.reshape(drows, 3 * inner)
    pack_b = jnp.concatenate(z_out + [section], axis=1)
    pack_c = jnp.concatenate(z_out2 + [w_up, w_down.T], axis=1)
    pack_d = jnp.concatenate(z_q2[1:], axis=1)
    full_a = lax.all_gather(pack_a, "seq", axis=0, tiled=True)
    full_b = lax.all_gather(pack_b, "seq", axis=0, tiled=True)
    full_c = lax.all_gather(pack_c, "seq", axis=0, tiled=True)
    full_d = lax.all_gather(pack_d, "seq", axis=0, tiled=True)
    full_kv = full_b[:, width : width + 2 * inner]
    own_out2 = full_c[:, :inner]

    scaled = jax.nn.silu(condition).astype(BF16)
    scaled_own = lax.dynamic_slice_in_dim(scaled, spot * drows, drows, 1)
    mod_part = seq_total(jnp.dot(scaled_own, w_ada, preferred_element_type=F32), nseq)
    mod_parts = tp_gather(mod_part, tp)
    mod_all = jnp.zeros((tp,) + mod_part.shape, F32)
    for k in range(tp):
        mod_all = lax.dynamic_update_index_in_dim(mod_all, mod_parts[k], (me - k) % tp, 0)
    mods = mod_all.transpose(1, 0, 2).reshape(clips, 6, width).transpose(1, 0, 2)
    mods = padded(mods, clip_pad, 1)

    def relative(value):
        parts = [
            lax.dynamic_slice_in_dim(value, ((me - k) % tp) * own_seqs, own_seqs, 0)
            for k in range(tp)
        ]
        return jnp.stack(parts)

    def row_form(value, fill=0):
        flat = relative(value).reshape((tp, own_seqs * fmax) + value.shape[2:])
        pads = [(0, 0), (0, own - own_seqs * fmax)] + [(0, 0)] * (flat.ndim - 2)
        flat = jnp.pad(flat, pads, constant_values=fill)
        return flat.reshape((rows,) + value.shape[2:])

    tok = row_form(tokens)
    cot = row_form(cotangent)
    ids = jnp.arange(clips)
    seq_hot = clip_of[:, None] == ids[None, :]
    seq_frames = jnp.sum(jnp.where(seq_hot, frames[None, :], 0), 1)
    live2 = jnp.arange(fmax)[None, :] < seq_frames[:, None]
    seq_index = jnp.broadcast_to(jnp.arange(seqs)[:, None], live2.shape)
    row_clip = row_form(jnp.broadcast_to(clip_of[:, None], live2.shape), -1)
    live = row_form(live2.astype(F32))[:, None]
    row_id = row_form(seq_index, -1)[:, None]
    key_id = row_form(jnp.where(live2, seq_index, -2), -2)[None, :]
    hot = (row_clip[:, None] == jnp.arange(clip_pad)[None, :]).astype(BF16)
    row_clip = row_clip[:, None]

    starts = jnp.cumsum(cap_len) - cap_len
    place = jnp.arange(keys)
    key_clip = jnp.sum((place[:, None] >= starts[None, :]).astype(jnp.int32), 1) - 1
    key_clip = jnp.where(place < jnp.sum(cap_len), key_clip, -9)[None, :]
    cap = jnp.zeros((keys + slots, width), BF16)
    for c in range(clips):
        cap = lax.dynamic_update_slice_in_dim(cap, caption[c], starts[c], 0)
    cap = jnp.where((place < jnp.sum(cap_len))[:, None], cap[:keys], 0)

    attn_in, qkv, probs, frame_out, frame_pack = call(
        functools.partial(frame_forward, tp),
        [
            sds((rows, width)),
            sds((rows, 3 * inner)),
            sds((heads, rows, rows)),
            sds((rows, inner)),
            sds((own, tp * inner)),
        ],
        tok,
        hot,
        mods,
        row_id,
        key_id,
        full_a,
        name="frame_forward",
    )
    (kv,) = call(
        key_values,
        [sds((keys, 2 * inner))],
        cap,
        full_kv,
        name="key_values",
    )
    frame_parts = tp_gather(frame_pack, tp)
    first, first_low, own_b1, cq, cprobs, cross_out, cross_pack = call(
        functools.partial(cross_forward, tp, inner),
        [
            sds((rows, width), F32),
            sds((rows, width)),
            sds((own, width), F32),
            sds((rows, inner)),
            sds((heads, rows, keys)),
            sds((rows, inner)),
            sds((own, tp * inner)),
        ],
        *frame_parts,
        tok,
        hot,
        mods,
        row_clip,
        key_clip,
        full_b,
        kv,
        name="cross_forward",
    )
    cross_parts = tp_gather(cross_pack, tp)
    outs = call(
        functools.partial(mlp_both, tp, inner),
        [sds((own, width), F32), sds((rows, width)), sds((rows, hid)), sds((rows, width)), sds((rows, hid))]
        + [sds((own, width))] * (2 * tp),
        *cross_parts,
        first,
        cot,
        live,
        hot,
        mods,
        full_c,
        name="mlp_both",
    )
    x2_own, mlp_in, hidden, d_b3, d_pre = outs[:5]
    b3_chunks, dm_chunks = outs[5 : 5 + tp], outs[5 + tp :]
    cot_own, live_own, hot_own, tok_own = cot[:own], live[:own], hot[:own], tok[:own]

    dm_parts = tp_scatter(dm_chunks, tp)
    g2_own, db2_own, sums_two = call(
        functools.partial(second_back, tp),
        [sds((own, width), F32), sds((own, width)), sds((2, clip_pad, width), F32)],
        *dm_parts,
        x2_own,
        cot_own,
        live_own,
        hot_own,
        mods,
        name="second_back",
    )
    (grad_one,) = call(
        weight_grads,
        [sds((width, 2 * hid))],
        mlp_in,
        d_pre,
        d_b3,
        hidden,
        name="grads_mlp",
    )
    sum_one = lax.psum_scatter(grad_one, "seq", scatter_dimension=0, tiled=True)
    db2_parts = tp_gather(db2_own, tp)
    d_b2, d_cq, d_kv, dcq_pack = call(
        functools.partial(cross_back, tp, inner),
        [sds((rows, width)), sds((rows, inner)), sds((keys, 2 * inner)), sds((own, tp * inner))],
        *db2_parts,
        own_out2,
        cprobs,
        kv,
        cq,
        name="cross_back",
    )
    dcq_parts = tp_gather(dcq_pack, tp)
    b3_parts = tp_scatter(b3_chunks, tp)
    out_own, sum_gate2 = call(
        functools.partial(out_rows, tp),
        [sds((own, width)), sds((clip_pad, width), F32)],
        *b3_parts,
        x2_own,
        cot_own,
        live_own,
        hot_own,
        mods,
        name="out_rows",
    )
    out_parts = tp_gather(out_own, tp)
    outs = call(
        functools.partial(frame_back, tp, inner),
        [
            sds((own, width), F32),
            sds((rows, width)),
            sds((rows, 3 * inner)),
            sds((3, clip_pad, width), F32),
        ]
        + [sds((own, width))] * tp,
        *dcq_parts,
        d_b2,
        g2_own,
        own_b1,
        tok,
        hot,
        mods,
        full_b,
        full_d,
        full_a,
        qkv,
        probs,
        name="frame_back",
    )
    g1_own, d_b1, d_qkv, sums_one = outs[:4]
    da_parts = tp_scatter(outs[4:], tp)
    (dtok_own,) = call(
        functools.partial(token_rows, tp),
        [sds((own, width))],
        *da_parts,
        tok_own,
        g1_own,
        hot_own,
        mods,
        name="token_rows",
    )
    dtok_parts = tp_gather(dtok_own, tp)

    def canonical(parts):
        whole = jnp.zeros((tp, own_seqs, fmax, width), BF16)
        for k in range(tp):
            part = parts[k][: own_seqs * fmax].reshape(own_seqs, fmax, width)
            whole = lax.dynamic_update_index_in_dim(whole, part, (me - k) % tp, 0)
        return whole.reshape(seqs, fmax, width)

    output = canonical(out_parts)
    d_tokens = canonical(dtok_parts)

    (grad_two,) = call(
        weight_grads,
        [sds((width, 4 * inner))],
        first_low,
        d_cq,
        cap,
        d_kv,
        d_b2,
        cross_out,
        name="grads_cross",
    )
    sum_two = lax.psum_scatter(grad_two, "seq", scatter_dimension=0, tiled=True)
    smem = pl.BlockSpec(memory_space=pltpu.SMEM)
    (grad_three,) = call(
        weight_grads_relative,
        [sds((nseq, drows, 4 * inner))],
        spot.reshape(1).astype(jnp.int32),
        attn_in,
        d_qkv,
        d_b1,
        frame_out,
        specs=[smem, None, None, None, None],
        name="grads_frame",
    )
    half = nseq // 2
    away = seq_xor(grad_three[half:], 1, nseq)
    near = (grad_three[:half].astype(F32) + away.astype(F32)).astype(BF16)
    sum_three = near[0].astype(F32)
    for c in range(1, half):
        sum_three = sum_three + seq_xor(near[c], 2 * c, nseq).astype(F32)

    grad_up = sum_one[:, :hid].astype(F32)
    grad_down = sum_one[:, hid:].astype(F32).T
    grad_q2 = sum_two[:, :inner].astype(F32)
    grad_kv2 = sum_two[:, inner : 3 * inner].astype(F32).reshape(drows, 2, inner)
    grad_out2 = sum_two[:, 3 * inner :].astype(F32).T
    grad_qkv = sum_three[:, : 3 * inner].reshape(drows, 3, inner)
    grad_out = sum_three[:, 3 * inner :].T

    kv_own = lax.psum_scatter(d_kv, "seq", scatter_dimension=0, tiled=True)
    feats = width // tp
    (cap_chunks,) = call(
        functools.partial(caption_rows, tp),
        [sds((tp, keys // nseq, feats))],
        me.reshape(1).astype(jnp.int32),
        kv_own,
        full_kv,
        specs=[smem, None, None],
        name="caption_rows",
    )
    cap_parts = tp_scatter([cap_chunks[r] for r in range(tp)], tp)
    cap_own = sum(p.astype(F32) for p in cap_parts).astype(BF16)
    cap_all = lax.all_gather(cap_own, "seq", axis=0, tiled=True)
    cap_all = jnp.pad(cap_all, ((0, slots), (0, 0)))
    d_caption = jnp.stack(
        [
            jnp.where(
                (jnp.arange(slots) < cap_len[c])[:, None],
                lax.dynamic_slice_in_dim(cap_all, starts[c], slots, 0).astype(F32),
                0.0,
            )
            for c in range(clips)
        ]
    )

    sums = jnp.stack(
        [sums_one[0], sums_one[1], sums_one[2], sums_two[0], sums_two[1], sum_gate2]
    )[:, :clips]
    d_mods = sums.transpose(1, 0, 2).reshape(clips, tp, 6 * width // tp)
    chunks = [lax.dynamic_index_in_dim(d_mods, (me - r) % tp, 1, False) for r in range(tp)]
    mod_cols = seq_total(sum(tp_scatter(chunks, tp)), nseq)
    grad_ada = lax.dot_general(
        scaled_own.astype(F32), mod_cols, (((0,), (0,)), ((), ())), precision=lax.Precision.HIGHEST
    )
    cond_part = lax.dot_general(
        mod_cols, w_ada.astype(F32), (((1,), (1,)), ((), ())), precision=lax.Precision.HIGHEST
    )
    cond_part = sum(tp_gather(cond_part, tp))
    cond_wide = lax.dynamic_update_slice_in_dim(
        jnp.zeros((clips, width), F32), cond_part, spot * drows, 1
    )
    cond_all = seq_total(cond_wide, nseq)
    d_condition = jax.vjp(jax.nn.silu, condition)[1](cond_all)[0]

    return (
        output,
        d_tokens,
        d_caption,
        d_condition,
        grad_qkv,
        grad_out,
        grad_q2,
        grad_kv2,
        grad_out2,
        grad_up,
        grad_down,
        grad_ada,
    )


def solution(mesh):
    return jax.shard_map(
        shards,
        mesh=mesh,
        in_specs=(
            P("seq", None, None),
            P("seq", None, None),
            P(),
            P(),
            P(),
            P(),
            P("seq"),
            P("seq", None, "tp"),
            P("tp", "seq"),
            P("seq", "tp"),
            P("seq", None, "tp"),
            P("tp", "seq"),
            P("seq", "tp"),
            P("tp", "seq"),
            P("seq", "tp"),
        ),
        out_specs=(
            P("seq", None, None),
            P("seq", None, None),
            P(None, None, "tp"),
            P(),
            P("seq", None, "tp"),
            P("tp", "seq"),
            P("seq", "tp"),
            P("seq", None, "tp"),
            P("tp", "seq"),
            P("seq", "tp"),
            P("tp", "seq"),
            P("seq", "tp"),
        ),
        check_vma=False,
    )
```

time: 1080 us -> 463 us (0.43)
  waiting for transfers between devices: 733 us -> 102 us
  matrix products: 105 us -> 4.47 us
  starting transfers between devices: 1.83 us -> 88.2 us
  blocking collectives: 95.8 us -> 10.5 us
  local copies, waits for them, and re-layouts: 71.9 us -> 144 us
  Pallas kernels: 0 us -> 54.1 us
  other arithmetic: 45.7 us -> 27.3 us
    psum x6 -> x0, waiting for transfers between devices: 412 us -> none  [the longest x5 407 us: total_rows(): return lax.psum(partial_value, 'tp')]
    reduce_scatter x7 -> x3, waiting for transfers between devices: 247 us -> 0.01 us  [the longest x1 0.01 us: shards(): kv_own = lax.psum_scatter(d_kv, 'seq', scatter_dimension=0, tiled=True)]
    ppermute x0 -> x55, waiting for transfers between devices: none -> 101 us  [the longest x27 45.1 us: tp_gather(): lax.ppermute(value, 'tp', [(i, (i + k) % tp) for i in range(tp)])]
    dot_general x37 -> x3, matrix products: 105 us -> 4.47 us  [the longest x1 2.35 us: shards(): lax.dot_general(scaled_own.astype(F32), mod_cols, (((0,), (0,)), ((), ())...]
    ppermute x0 -> x55, starting transfers between devices: none -> 87.7 us  [the longest x27 53.3 us: tp_gather(): lax.ppermute(value, 'tp', [(i, (i + k) % tp) for i in range(tp)])]
    all_gather x5 -> x4, waiting for transfers between devices: 71.1 us -> 0.04 us  [the longest x1 0.02 us: shards(): full_a = lax.all_gather(pack_a, 'seq', axis=0, tiled=True)]
    pallas_call x0 -> x13, Pallas kernels: none -> 54.1 us  [call(): pl.pallas_call(body, out_shape=tuple(outs), in_specs=in_specs, out_specs=...]
    all_gather x4 -> x1, blocking collectives: 53.3 us -> 10.5 us  [shards(): cap_all = lax.all_gather(cap_own, 'seq', axis=0, tiled=True)]
  transfers between devices with their start and end apart: 18 -> 62, of which waited for: 15 -> 27; matrix products, arithmetic and copies ran while one was open for 15% -> 26% of each run, Pallas kernels for 0% -> 12%
where the time goes in v1:
time: 463 us; the launch traced here: 454 us
  local copies, waits for them, and re-layouts  144 us (31%)
  waiting for transfers between devices  102 us (22%)
  starting transfers between devices  88.2 us (19%)
  Pallas kernels  54.1 us (12%)
  other arithmetic  27.3 us (6%)
  between operations  23.4 us (5%)
  blocking collectives  10.5 us (2%)
    unnamed x238, local copies, waits for them, and re-layouts  56.7 us
    pallas_call x13, Pallas kernels, call(): pl.pallas_call(body, out_shape=tuple(outs), in_specs=in_specs, out_specs=...  54.1 us
    ppermute x27, starting transfers between devices, tp_gather(): lax.ppermute(value, 'tp', [(i, (i + k) % tp) for i in range(tp)])  53.3 us
    ppermute x27, waiting for transfers between devices, tp_gather(): lax.ppermute(value, 'tp', [(i, (i + k) % tp) for i in range(tp)])  45.1 us
    ppermute x15, waiting for transfers between devices, tp_scatter(): lax.ppermute(chunks[r], 'tp', [(i, (i - r) % tp) for i in range(tp)])  38.1 us
    ppermute x15, starting transfers between devices, tp_scatter(): lax.ppermute(chunks[r], 'tp', [(i, (i - r) % tp) for i in range(tp)])  20.4 us
    ppermute x13, waiting for transfers between devices, seq_xor(): return lax.ppermute(value, 'seq', [(i, i ^ mask) for i in range(nseq)])  18.1 us
    dynamic_update_slice x4, local copies, waits for them, and re-layouts, shards(): cap = lax.dynamic_update_slice_in_dim(cap, caption[c], starts[c], 0)  15.9 us
  transfers between devices with their start and end apart: 62, of which 27 were waited for; matrix products, arithmetic and copies ran while one was open for 26% of the time, Pallas kernels for 12%

profile of v1, /device:TPU:0, one launch (start us, length us, event | category | flops | bytes accessed | tf_op | source)
XLA Modules:
  0.0 453.6 jit_solution(5661110061838152099)
XLA Ops:
  17.1 5.0 %collective-permute-done.9 = bf16[144,864]{1,0:T(8,128)(2,1)S(1)} collective-permute-done((bf16[144,864]{1,0:T(8,128)(2,1)S(1)}, bf16[144,864]{1,0:T(8,128)(2,1)S(1)}, u32[]{:S(2)}, u32[]{:S(2)}) %collective-permute-start.9) | collective-permute-done | bytes 248864 | tf_op jit(solution)/shard_map/ppermute | solution.py:310
  22.8 9.5 %collective-permute-done.10 = bf16[144,864]{1,0:T(8,128)(2,1)S(1)} collective-permute-done((bf16[144,864]{1,0:T(8,128)(2,1)S(1)}, bf16[144,864]{1,0:T(8,128)(2,1)S(1)}, u32[]{:S(2)}, u32[]{:S(2)}) %collective-permute-start.10) | collective-permute-done | bytes 248864 | tf_op jit(solution)/shard_map/ppermute | solution.py:310
  60.0 5.0 %fusion.36 = (bf16[1,300,1152]{2,0,1:T(2,128)(2,1)}, bf16[1,300,1152]{2,0,1:T(2,128)(2,1)}, bf16[1,300,1152]{2,0,1:T(2,128)(2,1)S(1)}, bf16[1,300,1152]{2,0,1:T(2,128)(2,1)S(1)}) fusion(bf16[4,300,1152]{2,0,1:T(4,128)(2,1)S(1)} %copy-done.80), kind=kLoop, calls=%fused_computation.137 | loop fusion | bytes 5529600 | tf_op jit(solution)/shard_map/slice | solution.py:430
  66.2 4.6 %dynamic_update_slice.59 = bf16[940,1152]{1,0:T(8,128)(2,1)S(1)} dynamic-update-slice(bf16[940,1152]{1,0:T(8,128)(2,1)S(1)} %broadcast_in_dim.144, bf16[300,1152]{1,0:T(8,128)(2,1)} %get-tuple-element.202, s32[]{:T(128)S(6)} %select_n.222, s32[]{:T(128)} %constant.171.clone.1) | dynamic-update-slice | bytes 1382404 | tf_op jit(solution)/shard_map/dynamic_update_slice | solution.py:430
  77.1 4.5 %dynamic_update_slice.61 = bf16[940,1152]{1,0:T(8,128)(2,1)S(1)} dynamic-update-slice(bf16[940,1152]{1,0:T(8,128)(2,1)S(1)} %dynamic_update_slice.60, bf16[300,1152]{1,0:T(8,128)(2,1)} %get-tuple-element.200, s32[]{:T(128)S(6)} %select_n.224, s32[]{:T(128)} %constant.171.clone.1) | dynamic-update-slice | bytes 1382404 | tf_op jit(solution)/shard_map/dynamic_update_slice | solution.py:430
  101.4 6.0 %collective-permute-start.3 = (f32[4,1728]{1,0:T(4,128)S(1)}, f32[4,1728]{1,0:T(4,128)S(1)}, u32[]{:S(2)}, u32[]{:S(2)}) collective-permute-start(f32[4,1728]{1,0:T(4,128)S(1)} %add.249), channel_id=1, source_target_pairs={{0,1},{1,2},{2,3},{3,0},{4,5},{5,6},{6,7},{7,4},{8,9},{9,10},{10,1... | collective-permute-start | bytes 82952 | tf_op jit(solution)/shard_map/ppermute | solution.py:310
  117.2 4.3 frame_forward.1
  137.5 8.3 %cross_forward.1 = (f32[288,1152]{1,0:T(8,128)S(1)}, bf16[288,1152]{1,0:T(8,128)(2,1)S(1)}, f32[72,1152]{1,0:T(8,128)S(1)}, bf16[288,288]{1,0:T(8,128)(2,1)S(1)}...) custom-call(bf16[72,1152]{1,0:T(8,128)(2,1)} %get-tuple-element.54.refs_0_, ...), custom_call_target="tpu_custom_call" | custom-call | bytes 11896960 | tf_op jit(solution)/shard_map/cross_forward/pallas_call | solution.py:36
  166.0 10.6 %mlp_both.1 = (f32[72,1152]{1,0:T(8,128)S(1)}, bf16[288,1152]{1,0:T(8,128)(2,1)S(1)}, bf16[288,1152]{1,0:T(8,128)(2,1)S(1)}, bf16[288,1152]{1,0:T(8,128)(2,1)S(1...) custom-call(bf16[72,1152]{1,0:T(8,128)(2,1)} %get-tuple-element.55.r, ...), custom_call_target="tpu_custom_call" | custom-call | bytes 15156864 | tf_op jit(solution)/shard_map/mlp_both/pallas_call | solution.py:36
  184.2 5.4 %collective-permute-start.21 = (bf16[72,1152]{1,0:T(8,128)(2,1)}, bf16[72,1152]{1,0:T(8,128)(2,1)S(1)}, u32[]{:S(2)}, u32[]{:S(2)}) collective-permute-start(bf16[72,1152]{1,0:T(8,128)(2,1)} %get-tuple-element.64), channel_id=1, source_target_pairs={{0,3},{1,0},{2,1},{3,2},{4,7},{5,4},{6,5},{7,6},{8,11},{9,8},{10,9... | collective-permute-start | bytes 497672 | tf_op jit(solution)/shard_map/ppermute | solution.py:316
  190.3 4.4 collective-permute-done.21.refs_1_
  194.7 9.9 %collective-permute-done.22.refs_2_ = bf16[72,1152]{1,0:T(8,128)(2,1)S(1)} collective-permute-done((bf16[72,1152]{1,0:T(8,128)(2,1)}, bf16[72,1152]{1,0:T(8,128)(2,1)S(1)}, u32[]{:S(2)}, u32[]{:S(2)}) %collective-permute-start.22) | collective-permute-done | bytes 165920 | tf_op jit(solution)/shard_map/ppermute | solution.py:316
  218.4 5.4 %collective-permute-done.25.refs_2_ = bf16[72,1152]{1,0:T(8,128)(2,1)S(1)} collective-permute-done((bf16[72,1152]{1,0:T(8,128)(2,1)S(1)}, bf16[72,1152]{1,0:T(8,128)(2,1)S(1)}, u32[]{:S(2)}, u32[]{:S(2)}) %collective-permute-start.25) | collective-permute-done | bytes 165920 | tf_op jit(solution)/shard_map/ppermute | solution.py:310
  223.8 4.0 cross_back.1
  235.8 4.3 grads_cross.1
  254.2 13.3 %collective-permute-done.16.refs_2_ = bf16[72,1152]{1,0:T(8,128)(2,1)S(1)} collective-permute-done((bf16[72,1152]{1,0:T(8,128)(2,1)}, bf16[72,1152]{1,0:T(8,128)(2,1)S(1)}, u32[]{:S(2)}, u32[]{:S(2)}) %collective-permute-start.16) | collective-permute-done | bytes 165920 | tf_op jit(solution)/shard_map/ppermute | solution.py:316
  278.3 11.1 %frame_back.1 = (f32[72,1152]{1,0:T(8,128)S(1)}, bf16[288,1152]{1,0:T(8,128)(2,1)S(1)}, bf16[288,864]{1,0:T(8,128)(2,1)S(1)}, f32[3,8,1152]{2,1,0:T(8,128)S(1)},...) custom-call(bf16[72,1152]{1,0:T(8,128)(2,1)S(1)} %copy-done.63, ...), custom_call_target="tpu_custom_call" | custom-call | bytes 15598080 | tf_op jit(solution)/shard_map/frame_back/pallas_call | solution.py:36
  308.5 5.4 %grads_mlp.1 = bf16[1152,2304]{1,0:T(8,128)(2,1)} custom-call(bf16[288,1152]{1,0:T(8,128)(2,1)S(1)} %copy-done.30, bf16[288,1152]{1,0:T(8,128)(2,1)S(1)} %copy-done.36, bf16[288,1152]{1,0:T(8,128)(2,1)S(1)} %copy-done.34, bf16[288,1152]{1,0:T(8,128)(2,1)S(1)} %copy-done.32), custom_call_target="tpu_custom_call" | custom-call | bytes 7962624 | tf_op jit(solution)/shard_map/grads_mlp/pallas_call | solution.py:36
  367.2 5.3 %collective-permute-done.31.refs_2_ = bf16[72,1152]{1,0:T(8,128)(2,1)S(1)} collective-permute-done((bf16[72,1152]{1,0:T(8,128)(2,1)}, bf16[72,1152]{1,0:T(8,128)(2,1)S(1)}, u32[]{:S(2)}, u32[]{:S(2)}) %collective-permute-start.31) | collective-permute-done | bytes 165920 | tf_op jit(solution)/shard_map/ppermute | solution.py:316
  383.7 5.7 %collective-permute-done.34 = bf16[72,1152]{1,0:T(8,128)(2,1)S(1)} collective-permute-done((bf16[72,1152]{1,0:T(8,128)(2,1)S(1)}, bf16[72,1152]{1,0:T(8,128)(2,1)S(1)}, u32[]{:S(2)}, u32[]{:S(2)}) %collective-permute-start.34) | collective-permute-done | bytes 165920 | tf_op jit(solution)/shard_map/ppermute | solution.py:310
  393.9 4.5 %collective-permute-start.36 = (bf16[80,288]{1,0:T(8,128)(2,1)}, bf16[80,288]{1,0:T(8,128)(2,1)S(1)}, u32[]{:S(2)}, u32[]{:S(2)}) collective-permute-start(bf16[80,288]{1,0:T(8,128)(2,1)} %get-tuple-element.164), channel_id=1, source_target_pairs={{0,3},{1,0},{2,1},{3,2},{4,7},{5,4},{6,5},{7,6},{8,11},{9,8},{10,9... | collective-permute-start | bytes 138248 | tf_op jit(solution)/shard_map/ppermute | solution.py:316
  405.7 10.5 %all_gather.19 = bf16[640,288]{1,0:T(8,128)(2,1)S(1)} all-gather(bf16[80,288]{1,0:T(8,128)(2,1)S(1)} %fusion.22), channel_id=1, replica_groups=mesh['seq'=8,'tp'=4] {'seq'}, dimensions={0}, use_global_device_ids=true | all-gather | bytes 414720 | tf_op jit(solution)/shard_map/all_gather | solution.py:643
  425.0 4.8 %collective-permute-done.52 = bf16[144,1152]{1,0:T(8,128)(2,1)S(1)} collective-permute-done((bf16[144,1152]{1,0:T(8,128)(2,1)}, bf16[144,1152]{1,0:T(8,128)(2,1)S(1)}, u32[]{:S(2)}, u32[]{:S(2)}) %collective-permute-start.52) | collective-permute-done | bytes 331808 | tf_op jit(solution)/shard_map/ppermute | solution.py:321
  429.8 7.8 %collective-permute-done.53 = bf16[144,1152]{1,0:T(8,128)(2,1)S(1)} collective-permute-done((bf16[144,1152]{1,0:T(8,128)(2,1)}, bf16[144,1152]{1,0:T(8,128)(2,1)S(1)}, u32[]{:S(2)}, u32[]{:S(2)}) %collective-permute-start.53) | collective-permute-done | bytes 331808 | tf_op jit(solution)/shard_map/ppermute | solution.py:321
  (527 shorter events, 270.5 us)
Async XLA Ops:
  7.2 107.7 %all-gather.5.cloned.1.call-start = ((), (), s32[]{:S(2)}) async-start(), calls=%async_computation.3 | async-start | bytes 2322432 | tf_op jit(solution)/shard_map/all_gather | solution.py:380
  9.5 120.6 %all-gather.7.cloned.1.call-start = ((), (), s32[]{:S(2)}) async-start(), calls=%async_computation.4 | async-start | bytes 5971968 | tf_op jit(solution)/shard_map/all_gather | solution.py:381
  12.8 19.4 %collective-permute-start.10 = (bf16[144,864]{1,0:T(8,128)(2,1)S(1)}, bf16[144,864]{1,0:T(8,128)(2,1)S(1)}, u32[]{:S(2)}, u32[]{:S(2)}) collective-permute-start(bf16[144,864]{1,0:T(8,128)(2,1)S(1)} %pad_maximum_fusion.1), channel_id=1, source_target_pairs={{0,2},{1,3},{2,0},{3,1},{4,6},{5,7},{6,4},{7,5},{8,10},{9,11},{10,... | collective-permute-start | bytes 746504 | tf_op jit(solution)/shard_map/ppermute | solution.py:310
  15.4 17.6 %collective-permute-start.11 = (bf16[144,864]{1,0:T(8,128)(2,1)S(1)}, bf16[144,864]{1,0:T(8,128)(2,1)S(1)}, u32[]{:S(2)}, u32[]{:S(2)}) collective-permute-start(bf16[144,864]{1,0:T(8,128)(2,1)S(1)} %pad_maximum_fusion.1), channel_id=1, source_target_pairs={{0,3},{1,0},{2,1},{3,2},{4,7},{5,4},{6,5},{7,6},{8,11},{9,8},{10,9... | collective-permute-start | bytes 746504 | tf_op jit(solution)/shard_map/ppermute | solution.py:310
  34.9 129.3 %all-gather.9.cloned.1.call-start = ((), (), s32[]{:S(2)}) async-start(), calls=%async_computation.5 | async-start | bytes 8957952 | tf_op jit(solution)/shard_map/all_gather | solution.py:382
  36.8 236.6 %all-gather.11.cloned.1.call-start = ((), (), s32[]{:S(2)}) async-start(), calls=%async_computation.6 | async-start | bytes 2322432 | tf_op jit(solution)/shard_map/all_gather | solution.py:383
  37.8 54.3 %collective-permute-start = (f32[4,1728]{1,0:T(4,128)}, f32[4,1728]{1,0:T(4,128)}, u32[]{:S(2)}, u32[]{:S(2)}) collective-permute-start(f32[4,1728]{1,0:T(4,128)} %fusion.44), channel_id=1, source_target_pairs={{0,4},{4,0},{8,12},{12,8},{16,20},{20,16},{24,28},{28,24},{1,5},{5... | collective-permute-start | bytes 82952 | tf_op jit(solution)/shard_map/ppermute | solution.py:321
  88.2 303.5 %reduce-scatter.4.cloned.1.call-start = ((), (), s32[]{:S(2)}) async-start(), calls=%async_computation.7 | async-start | bytes 921600 | tf_op jit(solution)/shard_map/reduce_scatter | solution.py:630
  189.6 15.0 %collective-permute-start.22 = (bf16[72,1152]{1,0:T(8,128)(2,1)}, bf16[72,1152]{1,0:T(8,128)(2,1)S(1)}, u32[]{:S(2)}, u32[]{:S(2)}) collective-permute-start(bf16[72,1152]{1,0:T(8,128)(2,1)} %get-tuple-element.65), channel_id=1, source_target_pairs={{0,2},{1,3},{2,0},{3,1},{4,6},{5,7},{6,4},{7,5},{8,10},{9,11},{10,... | collective-permute-start | bytes 497672 | tf_op jit(solution)/shard_map/ppermute | solution.py:316
  189.6 15.0 %collective-permute-start.23 = (bf16[72,1152]{1,0:T(8,128)(2,1)}, bf16[72,1152]{1,0:T(8,128)(2,1)S(1)}, u32[]{:S(2)}, u32[]{:S(2)}) collective-permute-start(bf16[72,1152]{1,0:T(8,128)(2,1)} %get-tuple-element.66), channel_id=1, source_target_pairs={{0,1},{1,2},{2,3},{3,0},{4,5},{5,6},{6,7},{7,4},{8,9},{9,10},{10,1... | collective-permute-start | bytes 497672 | tf_op jit(solution)/shard_map/ppermute | solution.py:316
  230.1 210.9 %reduce-scatter.6.cloned.1.call-start = ((), (), s32[]{:S(2)}) async-start(), calls=%async_computation.8 | async-start | bytes 2985984 | tf_op jit(solution)/shard_map/reduce_scatter | solution.py:602
  240.2 203.8 %reduce-scatter.8.cloned.1.call-start = ((), (), s32[]{:S(2)}) async-start(), calls=%async_computation.9 | async-start | bytes 5971968 | tf_op jit(solution)/shard_map/reduce_scatter | solution.py:518
  243.7 23.9 %collective-permute-start.16 = (bf16[72,1152]{1,0:T(8,128)(2,1)}, bf16[72,1152]{1,0:T(8,128)(2,1)S(1)}, u32[]{:S(2)}, u32[]{:S(2)}) collective-permute-start(bf16[72,1152]{1,0:T(8,128)(2,1)} %copy-done.78), channel_id=1, source_target_pairs={{0,2},{1,3},{2,0},{3,1},{4,6},{5,7},{6,4},{7,5},{8,10},{9,11},{10,... | collective-permute-start | bytes 497672 | tf_op jit(solution)/shard_map/ppermute | solution.py:316
  244.8 22.8 %collective-permute-start.17 = (bf16[72,1152]{1,0:T(8,128)(2,1)}, bf16[72,1152]{1,0:T(8,128)(2,1)S(1)}, u32[]{:S(2)}, u32[]{:S(2)}) collective-permute-start(bf16[72,1152]{1,0:T(8,128)(2,1)} %copy-done.77), channel_id=1, source_target_pairs={{0,1},{1,2},{2,3},{3,0},{4,5},{5,6},{6,7},{7,4},{8,9},{9,10},{10,1... | collective-permute-start | bytes 497672 | tf_op jit(solution)/shard_map/ppermute | solution.py:316
  244.8 28.6 %collective-permute-start.27 = (bf16[72,1152]{1,0:T(8,128)(2,1)}, bf16[72,1152]{1,0:T(8,128)(2,1)}, u32[]{:S(2)}, u32[]{:S(2)}) collective-permute-start(bf16[72,1152]{1,0:T(8,128)(2,1)} %copy-done.62), channel_id=1, source_target_pairs={{0,1},{1,2},{2,3},{3,0},{4,5},{5,6},{6,7},{7,4},{8,9},{9,10},{10,1... | collective-permute-start | bytes 497672 | tf_op jit(solution)/shard_map/ppermute | solution.py:310
  247.2 26.3 %collective-permute-start.28 = (bf16[72,1152]{1,0:T(8,128)(2,1)}, bf16[72,1152]{1,0:T(8,128)(2,1)}, u32[]{:S(2)}, u32[]{:S(2)}) collective-permute-start(bf16[72,1152]{1,0:T(8,128)(2,1)} %copy-done.62), channel_id=1, source_target_pairs={{0,2},{1,3},{2,0},{3,1},{4,6},{5,7},{6,4},{7,5},{8,10},{9,11},{10,... | collective-permute-start | bytes 497672 | tf_op jit(solution)/shard_map/ppermute | solution.py:310
  249.2 24.3 %collective-permute-start.29 = (bf16[72,1152]{1,0:T(8,128)(2,1)}, bf16[72,1152]{1,0:T(8,128)(2,1)}, u32[]{:S(2)}, u32[]{:S(2)}) collective-permute-start(bf16[72,1152]{1,0:T(8,128)(2,1)} %copy-done.62), channel_id=1, source_target_pairs={{0,3},{1,0},{2,1},{3,2},{4,7},{5,4},{6,5},{7,6},{8,11},{9,8},{10,9... | collective-permute-start | bytes 497672 | tf_op jit(solution)/shard_map/ppermute | solution.py:310
  304.5 14.7 %collective-permute-start.42 = (f32[4,1728]{1,0:T(4,128)}, f32[4,1728]{1,0:T(4,128)}, u32[]{:S(2)}, u32[]{:S(2)}) collective-permute-start(f32[4,1728]{1,0:T(4,128)} %fusion.25), channel_id=1, source_target_pairs={{0,4},{4,0},{8,12},{12,8},{16,20},{20,16},{24,28},{28,24},{1,5},{5... | collective-permute-start | bytes 82952 | tf_op jit(solution)/shard_map/ppermute | solution.py:321
  314.0 15.4 %collective-permute-start.19 = (bf16[72,1152]{1,0:T(8,128)(2,1)}, bf16[72,1152]{1,0:T(8,128)(2,1)S(1)}, u32[]{:S(2)}, u32[]{:S(2)}) collective-permute-start(bf16[72,1152]{1,0:T(8,128)(2,1)} %get-tuple-element.62), channel_id=1, source_target_pairs={{0,2},{1,3},{2,0},{3,1},{4,6},{5,7},{6,4},{7,5},{8,10},{9,11},{10,... | collective-permute-start | bytes 497672 | tf_op jit(solution)/shard_map/ppermute | solution.py:310
  315.3 24.7 %collective-permute-start.20 = (bf16[72,1152]{1,0:T(8,128)(2,1)}, bf16[72,1152]{1,0:T(8,128)(2,1)}, u32[]{:S(2)}, u32[]{:S(2)}) collective-permute-start(bf16[72,1152]{1,0:T(8,128)(2,1)} %get-tuple-element.62), channel_id=1, source_target_pairs={{0,3},{1,0},{2,1},{3,2},{4,7},{5,4},{6,5},{7,6},{8,11},{9,8},{10,9... | collective-permute-start | bytes 497672 | tf_op jit(solution)/shard_map/ppermute | solution.py:310
  355.8 60.4 %collective-permute-start.51 = (bf16[4,144,1152]{2,1,0:T(8,128)(2,1)}, bf16[4,144,1152]{2,1,0:T(8,128)(2,1)}, u32[]{:S(2)}, u32[]{:S(2)}) collective-permute-start(bf16[4,144,1152]{2,1,0:T(8,128)(2,1)} %slice.266), channel_id=1, source_target_pairs={{0,4},{4,0},{8,12},{12,8},{16,20},{20,16},{24,28},{28,24},{1,5},{5... | collective-permute-start | bytes 3981320 | tf_op jit(solution)/shard_map/ppermute | solution.py:321
  365.3 16.3 %collective-permute-start.50 = (f32[4,1152]{1,0:T(4,128)S(1)}, f32[4,1152]{1,0:T(4,128)S(1)}, u32[]{:S(2)}, u32[]{:S(2)}) collective-permute-start(f32[4,1152]{1,0:T(4,128)S(1)} %add.271), channel_id=1, source_target_pairs={{0,16},{4,20},{8,24},{12,28},{16,0},{20,4},{24,8},{28,12},{1,17},{... | collective-permute-start | bytes 55304 | tf_op jit(solution)/shard_map/ppermute | solution.py:321
  420.4 17.1 %collective-permute-start.53 = (bf16[144,1152]{1,0:T(8,128)(2,1)}, bf16[144,1152]{1,0:T(8,128)(2,1)S(1)}, u32[]{:S(2)}, u32[]{:S(2)}) collective-permute-start(bf16[144,1152]{1,0:T(8,128)(2,1)} %get-tuple-element.138), channel_id=1, source_target_pairs={{0,16},{4,20},{8,24},{12,28},{16,0},{20,4},{24,8},{28,12},{1,17},{... | collective-permute-start | bytes 995336 | tf_op jit(solution)/shard_map/ppermute | solution.py:321
  421.0 16.6 %collective-permute-start.54 = (bf16[144,1152]{1,0:T(8,128)(2,1)S(1)}, bf16[144,1152]{1,0:T(8,128)(2,1)}, u32[]{:S(2)}, u32[]{:S(2)}) collective-permute-start(bf16[144,1152]{1,0:T(8,128)(2,1)S(1)} %get-tuple-element.137), channel_id=1, source_target_pairs={{0,24},{4,28},{8,16},{12,20},{16,8},{20,12},{24,0},{28,4},{1,25},{... | collective-permute-start | bytes 995336 | tf_op jit(solution)/shard_map/ppermute | solution.py:321
  (154 other events, 931.0 us)
Sparse Core Ops, SparseCore 0:
  10.5 30.4 all-gather.4
  43.5 41.4 all-gather.6
  87.4 53.1 all-gather.8
  142.4 27.7 all-gather.10
  230.2 35.5 reduce-scatter.3
  269.5 43.7 reduce-scatter.5
  316.8 57.2 reduce-scatter.7
